TPU v7x, 256 devices: a whole 4x4x8 slice. The times are simulated.
256 devices in a mesh: ab: 64 (over z, y, core), cd: 4 (over x).
Axes of the slice: x: 4, y: 4, z: 8, core: 2. Of those that a mesh axis runs over, the one named last changes fastest.
Arguments:
- t2_amps: float32 [1024, 8192], P('ab', 'cd'), may hold values from -6 to 6
- v_slab: float32 [65536, 8192], P('ab', 'cd'), may hold values from -0.1875 to 0.1875
- ij_irrep: int32 [1024], P('ab'), may hold values from 0 to 7, as said below
- ab_irrep: int32 [65536], P('ab'), may hold values from 0 to 7, as said below
- cd_irrep: int32 [8192], P('cd'), may hold values from 0 to 7, as said below
Outputs:
- ladder: float32 [1024, 65536], P(('ab', 'cd'))
Inputs may be any that keep to these rules, and one draw needn't show every extreme that they name: `ij_irrep`: irrep labels of D2h in any order and any counts; a pair couples only to pairs of the same label. All occupied pairs of one device may carry one label. `ab_irrep`: irrep labels of D2h in any order and any counts; all pairs of one device may carry one label. `cd_irrep`: irrep labels of D2h in any order and any counts; all pairs of one device may carry one label.
All inputs are finite; a program needn't handle non-finite values.
Results may differ from a plain program's by a relative error of at most 0.0003.
Values sent between devices are 32-bit elements; how exact they have to be, the bound alone decides.
A program may use at most 64 MiB of HBM per device.

v0:
```python
import jax
import jax.numpy as jnp
from jax import lax
from jax.sharding import PartitionSpec as P


def on_device(t2_amps, v_slab, ij_irrep, ab_irrep, cd_irrep):
    t2_sym = t2_amps * (ij_irrep[:, None] == cd_irrep[None, :]).astype(t2_amps.dtype)
    v_sym = v_slab * (ab_irrep[:, None] == cd_irrep[None, :]).astype(v_slab.dtype)
    partial_value = lax.dot_general(
        lax.all_gather(t2_sym, "ab", axis=0, tiled=True),
        v_sym,
        (((1,), (1,)), ((), ())),
        precision=lax.Precision.HIGHEST,
        preferred_element_type=jnp.float32,
    )
    n_rows = lax.axis_size("ab")
    n_cols = lax.axis_size("cd")
    width = partial_value.shape[1]
    per_dev = partial_value.shape[0] // (n_rows * n_cols)
    regrouped = partial_value.reshape(n_rows, n_cols, per_dev, width)
    regrouped = jnp.transpose(regrouped, (1, 0, 2, 3)).reshape(partial_value.shape[0], width)
    summed = lax.psum_scatter(regrouped, "cd", scatter_dimension=0, tiled=True)
    ladder = lax.all_to_all(summed, "ab", split_axis=0, concat_axis=1, tiled=True)
    return ladder


def solution(mesh):
    in_specs = (P("ab", "cd"), P("ab", "cd"), P("ab"), P("ab"), P("cd"))
    out_specs = P(("ab", "cd"), None)
    return jax.shard_map(
        on_device, mesh=mesh, in_specs=in_specs, out_specs=out_specs, check_vma=False
    )
```

profile of v0, /device:TPU:1, one launch (start us, length us, event | category | flops | bytes accessed | tf_op | source)
XLA Modules:
  0.0 240.3 jit_solution(217428079767022441)
XLA Ops:
  6.5 0.0 all-gather.2.cloned.1.call-start
  6.5 1.7 compare_select_fusion
  8.2 0.0 all-gather.2.cloned.1.call-update
  8.2 0.0 reduce-scatter.2.cloned.1.call-start
  8.3 89.1 %all-gather.2.cloned.1.call-done = f32[1024,2048]{1,0:T(8,128)} async-done(((f32[16,2048]{1,0:T(8,128)}), f32[1024,2048]{1,0:T(8,128)}) %all-gather.2.cloned.1.call-update) | async-done | bytes 8388624 | tf_op jit(solution)/shard_map/all_gather | solution.py:11
  97.3 33.1 %fusion = f32[1024,1024]{1,0:T(8,128)} fusion(f32[1024,2048]{1,0:T(8,128)} %all-gather.2.cloned.1.call-done, f32[1024,2048]{1,0:T(8,128)} %param.6, s32[2048]{0:T(1024)} %param.9, s32[1024]{0:T(1024)} %param.8), kind=kOutput, calls=%fused_computation | convolution fusion | flops 25773998080 | bytes 20983808 | tf_op jit(solution)/shard_map/dot_general | solution.py:10
  130.4 5.2 %reshape.12 = f32[64,4,4,1024]{3,2,1,0:T(4,128)} reshape(f32[1024,1024]{1,0:T(8,128)} %fusion) | data formatting | bytes 8388608 | tf_op jit(solution)/shard_map/reshape | solution.py:21
  135.6 5.5 %copy.8 = f32[64,4,4,1024]{3,2,0,1:T(4,128)} copy(f32[64,4,4,1024]{3,2,1,0:T(4,128)} %reshape.12) | data formatting | bytes 8388608 | tf_op jit(solution)/shard_map/reshape | solution.py:21
  141.0 5.3 %reshape.13 = f32[1024,1024]{1,0:T(8,128)} reshape(f32[4,64,4,1024]{3,2,1,0:T(4,128)} %bitcast.7) | data formatting | bytes 8388608 | tf_op jit(solution)/shard_map/reshape | solution.py:22
  146.3 0.0 reduce-scatter.2.cloned.1.call-update
  146.4 45.8 %reduce-scatter.2.cloned.1.call-done = f32[256,1024]{1,0:T(8,128)} async-done(((f32[1024,1024]{1,0:T(8,128)}), f32[256,1024]{1,0:T(8,128)}) %reduce-scatter.2.cloned.1.call-update) | async-done | bytes 1048592 | tf_op jit(solution)/shard_map/reduce_scatter | solution.py:23
  192.2 1.5 all_to_all.14
  193.7 38.7 %all_to_all.19 = f32[64,4,1024]{2,1,0:T(4,128)S(1)} all-to-all(f32[64,4,1024]{2,1,0:T(4,128)S(1)} %all_to_all.14), channel_id=1, replica_groups=mesh['ab'=64,'cd'=4] {'ab'}, dimensions={0} | all-to-all | bytes 2097152 | tf_op jit(solution)/shard_map/all_to_all | solution.py:24
  232.4 1.0 copy.10
Async XLA Ops:
  6.5 90.8 %all-gather.2.cloned.1.call-start = ((), (), s32[]{:S(2)}) async-start(), calls=%async_computation.2 | async-start | bytes 8519680 | tf_op jit(solution)/shard_map/all_gather | solution.py:11
  8.2 184.0 %reduce-scatter.2.cloned.1.call-start = ((), (), s32[]{:S(2)}) async-start(), calls=%async_computation.3 | async-start | bytes 5242880 | tf_op jit(solution)/shard_map/reduce_scatter | solution.py:23
Sparse Core Ops, SparseCore 0:
  10.1 87.1 all-gather.1
  146.5 45.6 reduce-scatter.1
where the time goes:
time: 241 us; the launch traced here: 240 us
  waiting for transfers between devices  135 us (56%)
  blocking collectives  38.7 us (16%)
  matrix products  33.1 us (14%)
  local copies, waits for them, and re-layouts  18.4 us (8%)
  between operations  13.4 us (6%)
    all_gather x1, waiting for transfers between devices, on_device(): lax.all_gather(t2_sym, 'ab', axis=0, tiled=True)  89.1 us
    reduce_scatter x1, waiting for transfers between devices, on_device(): summed = lax.psum_scatter(regrouped, 'cd', scatter_dimension=0, tiled=True)  45.8 us
    all_to_all x1, blocking collectives, on_device(): lax.all_to_all(summed, 'ab', split_axis=0, concat_axis=1, tiled=True)  38.7 us
    dot_general x1, matrix products, on_device(): lax.dot_general(lax.all_gather(t2_sym, 'ab', axis=0, tiled=True), v_sym,...  33.1 us
    reshape x2, local copies, waits for them, and re-layouts, on_device(): regrouped = partial_value.reshape(n_rows, n_cols, per_dev, width)  10.6 us
    reshape x1, local copies, waits for them, and re-layouts, on_device(): jnp.transpose(regrouped, (1, 0, 2, 3))  5.29 us
  transfers between devices with their start and end apart: 2, of which 2 were waited for; matrix products, arithmetic and copies ran while one was open for 0% of the time, Pallas kernels for 0%

commit v1 on v0

v1 whole, which is shorter than its diff:
```python
import functools

import jax
import jax.numpy as jnp
from jax import lax
from jax.experimental import pallas as pl
from jax.experimental.pallas import tpu as pltpu
from jax.sharding import PartitionSpec as P

NZ, NY, NR, NX = 8, 4, 2, 4
NAB = NZ * NY * NR
ROWS = 16
CD = 2048
AB = 1024
W = CD + 128
LA = 1280
SLOTS = 72
CHUNKS = 2
WIDTH = AB // CHUNKS
HALF = WIDTH // 2
VROWS = 64
F32, BF16 = jnp.float32, jnp.bfloat16
MESH = pl.DeviceIdType.MESH


def pieces():
    size = {"a": LA / 2, "b": (W - LA) / 2}
    free = {}
    queue = []
    order = []

    def issue(now, link, item, amount):
        start = max(free.get(link, 0.0), now)
        free[link] = start + amount / 1000.0
        queue.append((free[link] + 2.0, len(order) + len(queue), link, item))

    def first(now, part, offset, axis):
        for sign in (1, -1):
            issue(now, axis + str(sign), (part, axis, offset, sign, 1), 2 * size[part])

    first(0.0, "a", 0, "z")
    first(0.0, "b", 0, "y")
    first(0.0, "b", 0, "z")
    first(0.0, "a", 0, "y")
    whole = {}
    while queue:
        queue.sort()
        now, _, link, item = queue.pop(0)
        order.append(item)
        part, axis, offset, sign, step = item
        last = 4 if axis == "z" else 2
        if step < last:
            half = step + 1 == last
            issue(now, link, (part, axis, offset, sign, step + 1), size[part] * (1 if half else 2))
        lead = (part == "a") == (axis == "z")
        if lead:
            if step < last:
                first(now, part, -sign * step, "y" if axis == "z" else "z")
            else:
                whole[part] = whole.get(part, 0) + 1
                if whole[part] == 2:
                    first(now, part, last, "y" if axis == "z" else "z")
    return order


ORDER = pieces()
INDEX = {item: n for n, item in enumerate(ORDER)}


def split2(x):
    hi = x.astype(BF16)
    return hi, (x - hi.astype(F32)).astype(BF16)


def dot_nt(a, b):
    return lax.dot_general(a, b, (((1,), (1,)), ((), ())), preferred_element_type=F32)


def column(row):
    n = row.shape[1]
    return jnp.concatenate(
        [jnp.transpose(jnp.broadcast_to(row[:, k : k + 128], (128, 128))) for k in range(0, n, 128)], axis=0
    )


def kernel(
    block_ref, v_ref, ab_ref, cd_ref, out_ref, flag_ref,
    g, vbuf, vhi, vlo, abcol, chi, part, landed, dense, place, tags,
    own_sem, v_sem, recv_sem, send_sem, mate_sem, x_send, x_recv, a_send, a_recv,
):
    ab = lax.axis_index("ab")
    x = lax.axis_index("cd")
    z, y, r = ab // 8, (ab // 2) % 4, ab % 2

    def name(zz, yy, rr):
        return ((zz % NZ) * NY + yy % NY) * NR + rr

    own = pltpu.make_async_copy(block_ref, g.at[ab], own_sem)
    own.start()

    def v_copy(n):
        return pltpu.make_async_copy(v_ref.at[pl.ds(n * VROWS, VROWS)], vbuf.at[n % 3], v_sem.at[n % 3])

    for n in range(2):
        v_copy(n).start()

    barrier = pltpu.get_barrier_semaphore()
    mates = [(name(z + 8 + s, y, r), x) for s in (1, -1)]
    mates += [(name(z, y + 4 + s, r), x) for s in (1, -1)]
    mates += [(name(z, y, 1 - r), x)]
    mates += [(ab, (x + d) % NX) for d in (1, 2, 3)]
    for mate in mates:
        pl.semaphore_signal(barrier, inc=1, device_id=mate, device_id_type=MESH)
    pl.semaphore_wait(barrier, len(mates))
    own.wait()

    lanes = {"a": pl.ds(0, LA), "b": pl.ds(LA, W - LA)}

    def piece(item):
        part_, axis, offset, sign, step = item
        rows = pl.ds(0, ROWS)
        if step == (4 if axis == "z" else 2):
            rows = pl.ds(0, 8) if sign == 1 else pl.ds(8, 8)
        if axis == "z":
            source = name(z + 16 - sign * (step - 1), y + 8 + offset, r)
            target = name(z + 16 + sign, y, r)
        else:
            source = name(z + 16 + offset, y + 8 - sign * (step - 1), r)
            target = name(z, y + 8 + sign, r)
        ref = g.at[source, rows, lanes[part_]]
        return pltpu.make_async_remote_copy(
            src_ref=ref, dst_ref=ref, send_sem=send_sem, recv_sem=recv_sem.at[INDEX[item]],
            device_id=(target, x), device_id_type=MESH,
        )

    def arrived(item):
        part_, axis, offset, sign, step = item
        rows = pl.ds(0, ROWS)
        if step == (4 if axis == "z" else 2):
            rows = pl.ds(0, 8) if sign == 1 else pl.ds(8, 8)
        if axis == "z":
            source = name(z + 16 - sign * step, y + 8 + offset, r)
        else:
            source = name(z + 16 + offset, y + 8 - sign * step, r)
        ref = g.at[source, rows, lanes[part_]]
        pltpu.make_async_copy(ref, ref, recv_sem.at[INDEX[item]]).wait()
        return source, rows

    def give(source, rows, part_):
        ref = g.at[source, rows] if part_ is None else g.at[source, rows, lanes[part_]]
        pltpu.make_async_remote_copy(
            src_ref=ref, dst_ref=ref, send_sem=send_sem, recv_sem=mate_sem,
            device_id=(name(z, y, 1 - r), x), device_id_type=MESH,
        ).start()

    def first(part_, offset, axis):
        for sign in (1, -1):
            piece((part_, axis, offset, sign, 1)).start()

    first("a", 0, "z")
    first("b", 0, "y")
    first("b", 0, "z")
    first("a", 0, "y")
    give(ab, pl.ds(0, ROWS), None)

    ab_row = ab_ref[...]
    cd_row = cd_ref[...]
    abcol[...] = column(ab_row)

    def v_step(n):
        if n + 2 < AB // VROWS:
            v_copy(n + 2).start()
        v_copy(n).wait()
        keep = abcol[n * VROWS : (n + 1) * VROWS, :1] == cd_row
        hi, lo = split2(jnp.where(keep, vbuf[n % 3], 0.0))
        vhi[n * VROWS : (n + 1) * VROWS, :] = hi
        vlo[n * VROWS : (n + 1) * VROWS, :] = lo

    steps = AB // VROWS
    done = 0
    whole = {}
    for count, item in enumerate(ORDER):
        part_, axis, offset, sign, step = item
        source, rows = arrived(item)
        last = 4 if axis == "z" else 2
        if step < last:
            piece((part_, axis, offset, sign, step + 1)).start()
        if (part_ == "a") == (axis == "z"):
            if step < last:
                first(part_, -sign * step, "y" if axis == "z" else "z")
            else:
                whole[part_] = whole.get(part_, 0) + 1
                if whole[part_] == 2:
                    first(part_, last, "y" if axis == "z" else "z")
        give(source, rows, part_)
        while done < steps and done * (len(ORDER) - 16) < count * steps:
            v_step(done)
            done += 1
    while done < steps:
        v_step(done)
        done += 1
    pltpu.make_async_copy(g.at[pl.ds(0, 32)], g.at[pl.ds(0, 32)], mate_sem).wait()

    row_i = lax.broadcasted_iota(jnp.int32, (512, 128), 0)
    lane_i = lax.broadcasted_iota(jnp.int32, (512, 128), 1)
    group = (row_i // 4) % 2
    below = (lax.broadcasted_iota(jnp.int32, (512, 512), 1) < lax.broadcasted_iota(jnp.int32, (512, 512), 0)).astype(BF16)
    slot_no = lax.broadcasted_iota(jnp.int32, (2 * SLOTS, 512), 0).astype(F32)
    cd_f = cd_row.astype(F32)
    most = jnp.zeros((1, 128), F32)
    for p in range(2):
        label = g[:, 8 * p : 8 * p + 8, CD:W].reshape(512, 128)
        one_hot = (label.astype(jnp.int32) + 8 * group == lane_i).astype(F32)
        before = jnp.dot(below, one_hot.astype(BF16), preferred_element_type=F32)
        slot = jnp.broadcast_to(jnp.sum(before * one_hot, axis=1, keepdims=True), (512, 128))
        most = jnp.maximum(most, jnp.max(slot, axis=0, keepdims=True))
        place[p] = slot.reshape(64, 8, 128)
        tags[p] = label.reshape(64, 8, 128)
        spot = jnp.transpose(slot + (SLOTS * group).astype(F32))[:1, :]
        pick = (slot_no == spot).astype(BF16)
        for k in range(0, CD, 512):
            amps = g[:, 8 * p : 8 * p + 8, k : k + 512].reshape(512, 512)
            hi, lo = split2(jnp.where(label[:, :1] == cd_f[:, k : k + 512], amps, 0.0))
            chi[2 * p * SLOTS : 2 * (p + 1) * SLOTS, k : k + 512] = jnp.dot(
                pick, hi, preferred_element_type=F32
            ).astype(BF16)
            chi[(4 + 2 * p) * SLOTS : (6 + 2 * p) * SLOTS, k : k + 512] = jnp.dot(
                pick, lo, preferred_element_type=F32
            ).astype(BF16)
    flag_ref[...] = jnp.broadcast_to(most, (8, 128))

    def x_copy(q, d):
        to = (x + d) % NX
        return pltpu.make_async_remote_copy(
            src_ref=part.at[q, to], dst_ref=landed.at[q, d - 1], send_sem=x_send.at[q, d - 1],
            recv_sem=x_recv.at[q, d - 1], device_id=(ab, to), device_id_type=MESH,
        )

    def product(q):
        cols = slice(q * WIDTH, (q + 1) * WIDTH)
        both = dot_nt(chi[...], vhi[cols, :])
        cross = dot_nt(chi[: 4 * SLOTS, :], vlo[cols, :])
        total = both[: 4 * SLOTS] + both[4 * SLOTS :] + cross
        for c in range(NX):
            part[q, c] = total[c * SLOTS : (c + 1) * SLOTS]
        for d in (2, 1, 3):
            x_copy(q, d).start()

    pair = x // 2
    half_r = lax.broadcasted_iota(jnp.int32, (64, 8, 128), 1) // 4

    def mine(ref):
        t = jnp.where(pair == 1, ref[1], ref[0])
        turned = jnp.concatenate([t[:, 4:, :], t[:, :4, :]], axis=1)
        return jnp.where(half_r == x % 2, t, turned).reshape(512, 128)

    product(0)
    my_slot = mine(place) + (SLOTS * group).astype(F32)
    my_label = mine(tags)
    ab_f = ab_row.astype(F32)
    lane2 = lax.broadcasted_iota(jnp.int32, (512, 2 * SLOTS), 1).astype(F32)
    spread = (my_slot[:, :1] == lane2).astype(BF16)

    def a_copy(q, d):
        dz, dy, dr = d // 8, (d // 2) % 4, d % 2
        to = name(z + dz, y + dy, (r + dr) % 2)
        return pltpu.make_async_remote_copy(
            src_ref=dense.at[q, to], dst_ref=out_ref.at[ab, :, pl.ds(q * HALF, HALF)], send_sem=a_send,
            recv_sem=a_recv, device_id=(to, x), device_id_type=MESH,
        )

    def exchange(q):
        for d in (1, 3, 2):
            x_copy(q, d).wait_recv()
        total = part[q, x] + landed[q, 0] + landed[q, 1] + landed[q, 2]
        even = [total[:, k : k + 128] for k in range(0, WIDTH, 256)]
        odd = [total[:, k + 128 : k + 256] for k in range(0, WIDTH, 256)]
        stacked = jnp.concatenate([jnp.concatenate(even, axis=1), jnp.concatenate(odd, axis=1)], axis=0)
        hi, rest = stacked.astype(BF16), None
        rest = stacked - hi.astype(F32)
        mid, lo = split2(rest)
        rows = jnp.dot(spread, hi, preferred_element_type=F32)
        rows = rows + jnp.dot(spread, mid, preferred_element_type=F32)
        rows = rows + jnp.dot(spread, lo, preferred_element_type=F32)
        base = q * WIDTH
        ab_even = jnp.concatenate([ab_f[:, base + k : base + k + 128] for k in range(0, WIDTH, 256)], axis=1)
        ab_odd = jnp.concatenate([ab_f[:, base + k + 128 : base + k + 256] for k in range(0, WIDTH, 256)], axis=1)
        wanted = jnp.where(group[:, :1] == 0, ab_even, ab_odd)
        rows = jnp.where(my_label[:, :1] == wanted, rows, 0.0)
        dense[q] = rows.reshape(64, 8, HALF)

        def send(d, carry):
            a_copy(q, d).start()
            return carry

        lax.fori_loop(1, NAB, send, 0)
        out_ref[ab, :, q * HALF : (q + 1) * HALF] = dense[q, ab]

    for q in range(CHUNKS):
        if q + 1 < CHUNKS:
            product(q + 1)
        exchange(q)

    for q in range(CHUNKS):
        for d in (1, 2, 3):
            x_copy(q, d).wait_send()
    pltpu.make_async_copy(g.at[pl.ds(0, 63)], g.at[pl.ds(0, 63)], send_sem).wait()
    everything = out_ref.at[pl.ds(0, NAB - 1)]
    pltpu.make_async_copy(everything, everything, a_send).wait()
    pltpu.make_async_copy(everything, everything, a_recv).wait()


def compact(t2_amps, v_slab, ij_irrep, ab_irrep, cd_irrep):
    labels = jnp.broadcast_to(ij_irrep.astype(F32)[:, None], (ROWS, 128))
    block = jnp.concatenate([t2_amps, labels], axis=1)
    vmem = pl.BlockSpec(memory_space=pltpu.VMEM)
    hbm = pl.BlockSpec(memory_space=pl.ANY)
    return pl.pallas_call(
        kernel,
        out_shape=(jax.ShapeDtypeStruct((NAB, 8, AB // 2), F32), jax.ShapeDtypeStruct((8, 128), F32)),
        in_specs=[hbm, hbm, vmem, vmem],
        out_specs=(vmem, vmem),
        scratch_shapes=[
            pltpu.VMEM((NAB, ROWS, W), F32),
            pltpu.VMEM((3, VROWS, CD), F32),
            pltpu.VMEM((AB, CD), BF16),
            pltpu.VMEM((AB, CD), BF16),
            pltpu.VMEM((AB, 128), jnp.int32),
            pltpu.VMEM((8 * SLOTS, CD), BF16),
            pltpu.VMEM((CHUNKS, NX, SLOTS, WIDTH), F32),
            pltpu.VMEM((CHUNKS, NX - 1, SLOTS, WIDTH), F32),
            pltpu.VMEM((CHUNKS, NAB, 8, HALF), F32),
            pltpu.VMEM((2, NAB, 8, 128), F32),
            pltpu.VMEM((2, NAB, 8, 128), F32),
            pltpu.SemaphoreType.DMA,
            pltpu.SemaphoreType.DMA((3,)),
            pltpu.SemaphoreType.DMA((len(ORDER),)),
            pltpu.SemaphoreType.DMA,
            pltpu.SemaphoreType.DMA,
            pltpu.SemaphoreType.DMA((CHUNKS, 3)),
            pltpu.SemaphoreType.DMA((CHUNKS, 3)),
            pltpu.SemaphoreType.DMA,
            pltpu.SemaphoreType.DMA,
        ],
        compiler_params=pltpu.CompilerParams(
            collective_id=0, has_side_effects=True, vmem_limit_bytes=56 * 1024 * 1024
        ),
    )(block, v_slab, ab_irrep[None, :], cd_irrep[None, :])


def dense_path(t2_amps, v_slab, ij_irrep, ab_irrep, cd_irrep):
    t2_sym = t2_amps * (ij_irrep[:, None] == cd_irrep[None, :]).astype(F32)
    v_sym = v_slab * (ab_irrep[:, None] == cd_irrep[None, :]).astype(F32)
    gathered = t2_sym
    hop = 1
    while hop < NAB:
        moved = lax.ppermute(gathered, "ab", [(i, (i + hop) % NAB) for i in range(NAB)])
        gathered = jnp.concatenate([moved, gathered], axis=0)
        hop *= 2
    me, x = lax.axis_index("ab"), lax.axis_index("cd")
    gathered = jnp.roll(gathered, (me + 1) * ROWS, axis=0)
    partial = lax.dot_general(
        gathered, v_sym, (((1,), (1,)), ((), ())), precision=lax.Precision.HIGHEST, preferred_element_type=F32
    )
    parts = jnp.transpose(partial.reshape(NAB, NX, ROWS // NX, AB), (1, 0, 2, 3))
    summed = lax.dynamic_index_in_dim(parts, x, 0, keepdims=False)
    for d in range(1, NX):
        theirs = lax.dynamic_index_in_dim(parts, (x + d) % NX, 0, keepdims=False)
        summed = summed + lax.ppermute(theirs, "cd", [(i, (i + d) % NX) for i in range(NX)])
    return lax.all_to_all(summed.reshape(NAB * ROWS // NX, AB), "ab", split_axis=0, concat_axis=1, tiled=True)


def on_device(t2_amps, v_slab, ij_irrep, ab_irrep, cd_irrep):
    rows, most = compact(t2_amps, v_slab, ij_irrep, ab_irrep, cd_irrep)

    def finish(rows, *_):
        tiles = rows.reshape(NAB, 2, 4, AB // 256, 128)
        return jnp.transpose(tiles, (2, 0, 3, 1, 4)).reshape(4, NAB * AB)

    def dense(_, *args):
        return dense_path(*args)

    return lax.cond(
        most[0, 0] >= SLOTS, dense, finish, rows, t2_amps, v_slab, ij_irrep, ab_irrep, cd_irrep
    )


def solution(mesh):
    in_specs = (P("ab", "cd"), P("ab", "cd"), P("ab"), P("ab"), P("cd"))
    return jax.shard_map(on_device, mesh=mesh, in_specs=in_specs, out_specs=P(("ab", "cd"), None), check_vma=False)
```

time: 241 us -> 94.7 us (0.39)
  waiting for transfers between devices: 135 us -> 0 us
  Pallas kernels: 0 us -> 86.9 us
  blocking collectives: 38.7 us -> 0 us
  matrix products: 33.1 us -> 0 us
  local copies, waits for them, and re-layouts: 18.4 us -> 4.17 us
  between operations: 13.4 us -> 0.72 us
    all_gather x1 -> x0, waiting for transfers between devices: 89.1 us -> none  [on_device(): lax.all_gather(t2_sym, 'ab', axis=0, tiled=True)]
    pallas_call x0 -> x1, Pallas kernels: none -> 86.9 us  [compact(): pl.pallas_call(kernel, out_shape=(jax.ShapeDtypeStruct((NAB, 8, AB // 2),...]
    reduce_scatter x1 -> x0, waiting for transfers between devices: 45.8 us -> none  [on_device(): summed = lax.psum_scatter(regrouped, 'cd', scatter_dimension=0, tiled=True)]
    all_to_all x1 -> x0, blocking collectives: 38.7 us -> none  [on_device(): lax.all_to_all(summed, 'ab', split_axis=0, concat_axis=1, tiled=True)]
    dot_general x1 -> x0, matrix products: 33.1 us -> none  [on_device(): lax.dot_general(lax.all_gather(t2_sym, 'ab', axis=0, tiled=True), v_sym,...]
    reshape x3, local copies, waits for them, and re-layouts: 15.9 us -> 1.92 us  [the longest x1 1.02 us: finish(): return jnp.transpose(tiles, (2, 0, 3, 1, 4)).reshape(4, NAB * AB)]
  transfers between devices with their start and end apart: 2 -> 0, of which waited for: 2 -> 0; matrix products, arithmetic and copies ran while one was open for 0% -> 0% of each run, Pallas kernels for 0% -> 0%
where the time goes in v1:
time: 94.7 us; the launch traced here: 94.5 us
  Pallas kernels  86.9 us (92%)
  local copies, waits for them, and re-layouts  4.17 us (4%)
  other arithmetic  2.28 us (2%)
    pallas_call x1, Pallas kernels, compact(): pl.pallas_call(kernel, out_shape=(jax.ShapeDtypeStruct((NAB, 8, AB // 2),...  86.9 us

profile of v1, /device:TPU:1, one launch (start us, length us, event | category | flops | bytes accessed | tf_op | source)
XLA Modules:
  0.0 94.5 jit_solution(17274587040511252941)
XLA Ops:
  0.0 0.0 copy-start.6
  0.0 0.0 copy-start.2
  0.0 0.0 copy-start.7
  0.0 0.0 copy-start.5
  0.0 0.7 convert_element_type.11
  0.7 0.1 broadcast_in_dim.6
  0.8 1.6 %pad_maximum_fusion.3.block_ref = f32[16,2176]{1,0:T(8,128)} fusion(f32[16,128]{1,0:T(8,128)S(1)} %broadcast_in_dim.6, f32[16,2048]{1,0:T(8,128)} %param.7), kind=kLoop, calls=%fused_computation.50 | loop fusion | flops 34816 | bytes 278528 | tf_op jit(solution)/shard_map/concatenate | solution.py:315
  2.4 86.9 %shard_map.57 = (f32[64,8,512]{2,1,0:T(8,128)S(1)}, f32[8,128]{1,0:T(8,128)}) custom-call(f32[16,2176]{1,0:T(8,128)} %pad_maximum_fusion.3.block_ref, f32[1024,2048]{1,0:T(8,128)} %v_ref.1, s32[1,1024]{1,0:T(1,128)} %bitcast.34, s32[1,2048]{1,0:T(1,128)} %bitcast.33), custom_call_target="tpu_custom_call" | custom-call | tf_op jit(solution)/shard_map/pallas_call | solution.py:318
  89.2 1.2 %slice.3 = f32[1,1]{1,0:T(1,128)} slice(f32[8,128]{1,0:T(8,128)} %get-tuple-element.26), slice={[0:1], [0:1]} | slice | bytes 8 | tf_op jit(solution)/shard_map/slice | solution.py:384
  91.1 0.0 copy-done.6
  91.1 0.0 copy-done.2
  91.1 0.0 copy-done.7
  91.1 0.0 copy-done.5
  91.1 2.4 %conditional.1 = (f32[4,65536]{1,0:T(4,128)S(1)}) conditional(s32[]{:T(128)} %bitcast.9, f32[64,8,512]{2,1,0:T(8,128)S(1)} %get-tuple-element.27, (s32[16]{0:T(128)S(1)}, s32[2048]{0:T(1024)S(1)}, f32[16,2048]{1,0:T(8,128)S(1)}, s32[1024]{0:T(1024)S(1)}, f32[1024,2048]{1,0:T(8,128)}) %tuple.22), branch_computations={%region_0.0_spmd, %region_1.2_spmd} | conditional | flops 25776226304 | bytes 179624960 | solution.py:383
  91.3 0.4 reshape.27
  91.7 0.5 copy.35
  92.2 1.0 %reshape.28 = f32[4,65536]{1,0:T(4,128)S(1)} reshape(f32[4,64,4,2,128]{4,3,2,1,0:T(2,128)S(1)} %bitcast.29) | data formatting | bytes 2097152 | tf_op jit(solution)/shard_map/cond/branch_0_fun/reshape | solution.py:378
  93.5 1.0 %copy.64 = f32[4,65536]{1,0:T(4,128)} copy(f32[4,65536]{1,0:T(4,128)S(1)} %get-tuple-element.28) | data formatting | bytes 2097152
Async XLA Ops:
  0.0 91.1 %copy-start.6 = (s32[16]{0:T(128)S(1)}, s32[16]{0:T(128)}, u32[]{:S(2)}) copy-start(s32[16]{0:T(128)} %param.9) | copy-start | bytes 196
  0.0 91.1 %copy-start.2 = (f32[16,2048]{1,0:T(8,128)S(1)}, f32[16,2048]{1,0:T(8,128)}, u32[]{:S(2)}) copy-start(f32[16,2048]{1,0:T(8,128)} %param.7) | copy-start | bytes 393220
  0.0 91.1 %copy-start.7 = (s32[1024]{0:T(1024)S(1)}, s32[1024]{0:T(1024)}, u32[]{:S(2)}) copy-start(s32[1024]{0:T(1024)} %param.10) | copy-start | bytes 12292
  0.0 91.1 %copy-start.5 = (s32[2048]{0:T(1024)S(1)}, s32[2048]{0:T(1024)}, u32[]{:S(2)}) copy-start(s32[2048]{0:T(1024)} %param.11) | copy-start | bytes 24580

commit v2 on v1

v2 whole, which is shorter than its diff:
```python
import functools

import jax
import jax.numpy as jnp
from jax import lax
from jax.experimental import pallas as pl
from jax.experimental.pallas import tpu as pltpu
from jax.sharding import PartitionSpec as P

NZ, NY, NR, NX = 8, 4, 2, 4
NAB = NZ * NY * NR
ROWS = 16
CD = 2048
AB = 1024
SLOTS = 72
LEAD = 40
CHUNKS = 4
WIDTH = AB // CHUNKS
VROWS = 64
GROUP = NAB * 4
F32, BF16 = jnp.float32, jnp.bfloat16
MESH = pl.DeviceIdType.MESH
EARLY = 10
SPAN = {"a": (0, 24, LEAD), "b": (LEAD, 56, SLOTS)}


def span(part, step, axis, sign):
    low, middle, high = SPAN[part]
    if step < (4 if axis == "z" else 2):
        return low, high - low
    return (low, middle - low) if sign == 1 else (middle, high - middle)


def pieces():
    free = {}
    queue = []
    order = []

    def issue(now, item):
        part, axis, _, sign, step = item
        link = axis + str(sign)
        start = max(free.get(link, 0.0), now)
        free[link] = start + span(part, step, axis, sign)[1] * 0.0111
        queue.append((free[link] + 1.8, len(order) + len(queue), item))

    def first(now, part, offset, axis):
        for sign in (1, -1):
            issue(now, (part, axis, offset, sign, 1))

    first(0.0, "a", 0, "z")
    first(0.0, "b", 0, "y")
    first(0.0, "b", 0, "z")
    first(0.0, "a", 0, "y")
    whole = {}
    while queue:
        queue.sort()
        now, _, item = queue.pop(0)
        order.append(item)
        part, axis, offset, sign, step = item
        last = 4 if axis == "z" else 2
        if step < last:
            issue(now, (part, axis, offset, sign, step + 1))
        if (part == "a") == (axis == "z"):
            if step < last:
                first(now, part, -sign * step, "y" if axis == "z" else "z")
            else:
                whole[part] = whole.get(part, 0) + 1
                if whole[part] == 2:
                    first(now, part, last, "y" if axis == "z" else "z")
    return order


ORDER = pieces()
INDEX = {item: n for n, item in enumerate(ORDER)}


def split2(x):
    hi = x.astype(BF16)
    return hi, (x - hi.astype(F32)).astype(BF16)


def dot_nt(a, b):
    return lax.dot_general(a, b, (((1,), (1,)), ((), ())), preferred_element_type=F32)


def dot(a, b):
    return jnp.dot(a, b, preferred_element_type=F32)


def column(row):
    n = row.shape[1]
    return jnp.concatenate(
        [jnp.transpose(jnp.broadcast_to(row[:, k : k + 128], (128, 128))) for k in range(0, n, 128)], axis=0
    )


def kernel(
    t2_ref, v_ref, ij_ref, ab_ref, cd_ref, chunk_ref, out_ref, flag_ref,
    amps, amps4, mine, labels, rows4, g, vbuf, vhi, vlo, abcol, chi, part, landed, dense,
    own_sem, v_sem, s_send, q_recv, l_recv, recv_sem, send_sem, mate_sem, x_send, x_recv, a_send, a_recv,
):
    ab = lax.axis_index("ab")
    x = lax.axis_index("cd")
    z, y, r = ab // 8, (ab // 2) % 4, ab % 2

    def name(zz, yy, rr):
        return ((zz % NZ) * NY + yy % NY) * NR + rr

    def peer(d):
        return z + d // 8, y + (d // 2) % 4, (r + d % 2) % 2

    load = pltpu.make_async_copy(t2_ref, amps, own_sem.at[0])
    load.start()

    def v_copy(n):
        return pltpu.make_async_copy(v_ref.at[pl.ds(n * VROWS, VROWS)], vbuf.at[n % 3], v_sem.at[n % 3])

    barrier = pltpu.get_barrier_semaphore()

    def greet(d, carry):
        pl.semaphore_signal(barrier, inc=1, device_id=(name(*peer(d)), x), device_id_type=MESH)
        return carry

    lax.fori_loop(1, NAB, greet, 0)
    for d in (1, 2, 3):
        pl.semaphore_signal(barrier, inc=1, device_id=(ab, (x + d) % NX), device_id_type=MESH)

    mine[...] = jnp.full((1, 128), -1, jnp.int32)
    mine[:, :ROWS] = ij_ref[...]
    load.wait()
    for n in range(2):
        v_copy(n).start()
    for c in range(NX):
        amps4[c] = amps[4 * c : 4 * c + 4, :]
    pl.semaphore_wait(barrier, NAB - 1 + NX - 1)

    def scatter(d, carry):
        zz, yy, rr = peer(d)
        zz, yy = zz % NZ, yy % NY
        to = (name(zz, yy, rr), x)
        pltpu.make_async_remote_copy(
            src_ref=mine, dst_ref=labels.at[ab], send_sem=s_send.at[0], recv_sem=l_recv, device_id=to, device_id_type=MESH
        ).start()
        pltpu.make_async_remote_copy(
            src_ref=amps4.at[yy, :, pl.ds(pl.multiple_of((zz * 2 + rr) * 128, 128), 128)], dst_ref=rows4.at[ab],
            send_sem=s_send.at[1], recv_sem=q_recv, device_id=to, device_id_type=MESH,
        ).start()
        return carry

    lax.fori_loop(1, NAB, scatter, 0)
    keep_label = pltpu.make_async_copy(mine, labels.at[ab], own_sem.at[1])
    keep_rows = pltpu.make_async_copy(
        amps4.at[y, :, pl.ds(pl.multiple_of((z * 2 + r) * 128, 128), 128)], rows4.at[ab], own_sem.at[2]
    )
    keep_label.start()
    keep_rows.start()

    ab_row = ab_ref[...]
    cd_row = cd_ref[...]
    abcol[...] = column(ab_row)

    def v_step(n):
        if n + 2 < AB // VROWS:
            v_copy(n + 2).start()
        v_copy(n).wait()
        keep = abcol[n * VROWS : (n + 1) * VROWS, :1] == cd_row
        hi, lo = split2(jnp.where(keep, vbuf[n % 3], 0.0))
        vhi[n * VROWS : (n + 1) * VROWS, :] = hi
        vlo[n * VROWS : (n + 1) * VROWS, :] = lo

    for n in range(EARLY):
        v_step(n)

    row_i = lax.broadcasted_iota(jnp.int32, (GROUP, 128), 0)
    lane_i = lax.broadcasted_iota(jnp.int32, (GROUP, 128), 1)
    square = (GROUP, GROUP)
    below = (lax.broadcasted_iota(jnp.int32, square, 1) < lax.broadcasted_iota(jnp.int32, square, 0)).astype(BF16)
    repeat = (
        lax.broadcasted_iota(jnp.int32, (GROUP, NAB), 1) == lax.broadcasted_iota(jnp.int32, (GROUP, NAB), 0) // 4
    ).astype(BF16)

    keep_label.wait()
    others = pl.ds(0, NAB - 1)
    pltpu.make_async_copy(labels.at[others], labels.at[others], l_recv).wait()
    table = labels[...].reshape(NAB, 128).astype(F32).astype(BF16)
    by_row = dot(repeat, table)

    def slots_of(c):
        label = jnp.sum(jnp.where(lane_i == 4 * c + row_i % 4, by_row, 0.0), axis=1, keepdims=True)
        one_hot = jnp.where(label == lane_i.astype(F32), 1.0, 0.0)
        before = dot(below, one_hot.astype(BF16))
        slot = jnp.sum(before * one_hot, axis=1, keepdims=True)
        return jnp.broadcast_to(label, (GROUP, 128)), jnp.broadcast_to(slot, (GROUP, 128))

    label_y, slot_y = slots_of(y)
    spot = jnp.transpose(slot_y)[:1, :]
    pick = (lax.broadcasted_iota(jnp.int32, (SLOTS, GROUP), 0).astype(F32) == spot).astype(BF16)
    my_cd = chunk_ref[pl.ds(2 * z + r, 1), :].astype(F32)
    keep_rows.wait()
    pltpu.make_async_copy(rows4.at[others], rows4.at[others], q_recv).wait()
    hi, lo = split2(jnp.where(label_y == my_cd, rows4[...].reshape(GROUP, 128), 0.0))
    g[ab] = dot(pick, hi) + dot(pick, lo)

    def sent(item):
        part_, axis, offset, sign, step = item
        low, count = span(part_, step, axis, sign)
        if axis == "z":
            source = name(z + 16 - sign * (step - 1), y + 8 + offset, r)
            target = name(z + 16 + sign, y, r)
        else:
            source = name(z + 16 + offset, y + 8 - sign * (step - 1), r)
            target = name(z, y + 8 + sign, r)
        ref = g.at[source, pl.ds(low, count)]
        return pltpu.make_async_remote_copy(
            src_ref=ref, dst_ref=ref, send_sem=send_sem, recv_sem=recv_sem.at[INDEX[item]],
            device_id=(target, x), device_id_type=MESH,
        )

    def arrived(item):
        part_, axis, offset, sign, step = item
        if axis == "z":
            source = name(z + 16 - sign * step, y + 8 + offset, r)
        else:
            source = name(z + 16 + offset, y + 8 - sign * step, r)
        rows = pl.ds(*span(part_, step, axis, sign))
        ref = g.at[source, rows]
        pltpu.make_async_copy(ref, ref, recv_sem.at[INDEX[item]]).wait()
        return source, rows

    def give(source, rows):
        ref = g.at[source, rows]
        pltpu.make_async_remote_copy(
            src_ref=ref, dst_ref=ref, send_sem=send_sem, recv_sem=mate_sem,
            device_id=(name(z, y, 1 - r), x), device_id_type=MESH,
        ).start()

    def first(part_, offset, axis):
        for sign in (1, -1):
            sent((part_, axis, offset, sign, 1)).start()

    first("a", 0, "z")
    first("b", 0, "y")
    first("b", 0, "z")
    first("a", 0, "y")
    give(ab, pl.ds(0, SLOTS))

    most = jnp.zeros((1, 128), F32)
    my_label = jnp.zeros((GROUP, 128), F32)
    my_slot = jnp.zeros((GROUP, 128), F32)
    for c in range(NX):
        label, slot = slots_of(c)
        most = jnp.maximum(most, jnp.max(slot, axis=0, keepdims=True))
        my_label = jnp.where(x == c, label, my_label)
        my_slot = jnp.where(x == c, slot, my_slot)
    flag_ref[...] = jnp.broadcast_to(most, (8, 128))
    spread = (my_slot[:, :SLOTS] == lane_i[:, :SLOTS].astype(F32)).astype(BF16)

    steps = AB // VROWS
    done = EARLY
    whole = {}
    for count, item in enumerate(ORDER):
        part_, axis, offset, sign, step = item
        source, rows = arrived(item)
        last = 4 if axis == "z" else 2
        if step < last:
            sent((part_, axis, offset, sign, step + 1)).start()
        if (part_ == "a") == (axis == "z"):
            if step < last:
                first(part_, -sign * step, "y" if axis == "z" else "z")
            else:
                whole[part_] = whole.get(part_, 0) + 1
                if whole[part_] == 2:
                    first(part_, last, "y" if axis == "z" else "z")
        give(source, rows)
        while done < steps and (done - EARLY) * (len(ORDER) - 16) < count * (steps - EARLY):
            v_step(done)
            done += 1
    while done < steps:
        v_step(done)
        done += 1
    pltpu.make_async_copy(g.at[pl.ds(0, 32)], g.at[pl.ds(0, 32)], mate_sem).wait()

    for k in range(CD // 128):
        block = jnp.concatenate([g[((k // 2) * NY + c) * NR + k % 2] for c in range(NX)], axis=0)
        hi, lo = split2(block)
        chi[: NX * SLOTS, k * 128 : (k + 1) * 128] = hi
        chi[NX * SLOTS :, k * 128 : (k + 1) * 128] = lo

    def x_copy(q, d):
        to = (x + d) % NX
        return pltpu.make_async_remote_copy(
            src_ref=part.at[q, to], dst_ref=landed.at[q, d - 1], send_sem=x_send.at[q, d - 1],
            recv_sem=x_recv.at[q, d - 1], device_id=(ab, to), device_id_type=MESH,
        )

    def product(q):
        cols = slice(q * WIDTH, (q + 1) * WIDTH)
        both = dot_nt(chi[...], vhi[cols, :])
        cross = dot_nt(chi[: NX * SLOTS, :], vlo[cols, :])
        total = both[: NX * SLOTS] + both[NX * SLOTS :] + cross
        for c in range(NX):
            part[q, c] = total[c * SLOTS : (c + 1) * SLOTS]
        for d in (2, 1, 3):
            x_copy(q, d).start()

    ab_f = ab_row.astype(F32)

    def exchange(q):
        cols = slice(q * WIDTH, (q + 1) * WIDTH)
        for d in (1, 3, 2):
            x_copy(q, d).wait_recv()
        total = part[q, x] + landed[q, 0] + landed[q, 1] + landed[q, 2]
        hi = total.astype(BF16)
        mid, lo = split2(total - hi.astype(F32))
        rows = dot(spread, hi) + dot(spread, mid) + dot(spread, lo)
        rows = jnp.where(my_label[:, :1] == ab_f[:, cols], rows, 0.0)
        dense[q] = rows.reshape(NAB, 4, WIDTH)

        def send(d, carry):
            to = name(*peer(d))
            pltpu.make_async_remote_copy(
                src_ref=dense.at[q, to], dst_ref=out_ref.at[ab, :, pl.ds(q * WIDTH, WIDTH)], send_sem=a_send,
                recv_sem=a_recv, device_id=(to, x), device_id_type=MESH,
            ).start()
            return carry

        lax.fori_loop(1, NAB, send, 0)
        out_ref[ab, :, cols] = dense[q, ab]

    product(0)
    for q in range(CHUNKS):
        if q + 1 < CHUNKS:
            product(q + 1)
        exchange(q)

    for q in range(CHUNKS):
        for d in (1, 2, 3):
            x_copy(q, d).wait_send()
    pltpu.make_async_copy(labels.at[others], labels.at[others], s_send.at[0]).wait()
    pltpu.make_async_copy(rows4.at[others], rows4.at[others], s_send.at[1]).wait()
    pltpu.make_async_copy(g.at[others], g.at[others], send_sem).wait()
    pltpu.make_async_copy(out_ref.at[others], out_ref.at[others], a_send).wait()
    pltpu.make_async_copy(out_ref.at[others], out_ref.at[others], a_recv).wait()


def compact(t2_amps, v_slab, ij_irrep, ab_irrep, cd_irrep):
    vmem = pl.BlockSpec(memory_space=pltpu.VMEM)
    hbm = pl.BlockSpec(memory_space=pl.ANY)
    return pl.pallas_call(
        kernel,
        out_shape=(jax.ShapeDtypeStruct((NAB, 4, AB), F32), jax.ShapeDtypeStruct((8, 128), F32)),
        in_specs=[hbm, hbm, vmem, vmem, vmem, vmem],
        out_specs=(vmem, vmem),
        scratch_shapes=[
            pltpu.VMEM((ROWS, CD), F32),
            pltpu.VMEM((NX, 4, CD), F32),
            pltpu.VMEM((1, 128), jnp.int32),
            pltpu.VMEM((NAB, 1, 128), jnp.int32),
            pltpu.VMEM((NAB, 4, 128), F32),
            pltpu.VMEM((NAB, SLOTS, 128), F32),
            pltpu.VMEM((3, VROWS, CD), F32),
            pltpu.VMEM((AB, CD), BF16),
            pltpu.VMEM((AB, CD), BF16),
            pltpu.VMEM((AB, 128), jnp.int32),
            pltpu.VMEM((2 * NX * SLOTS, CD), BF16),
            pltpu.VMEM((CHUNKS, NX, SLOTS, WIDTH), F32),
            pltpu.VMEM((CHUNKS, NX - 1, SLOTS, WIDTH), F32),
            pltpu.VMEM((CHUNKS, NAB, 4, WIDTH), F32),
            pltpu.SemaphoreType.DMA((3,)),
            pltpu.SemaphoreType.DMA((3,)),
            pltpu.SemaphoreType.DMA((2,)),
            pltpu.SemaphoreType.DMA,
            pltpu.SemaphoreType.DMA,
            pltpu.SemaphoreType.DMA((len(ORDER),)),
            pltpu.SemaphoreType.DMA,
            pltpu.SemaphoreType.DMA,
            pltpu.SemaphoreType.DMA((CHUNKS, 3)),
            pltpu.SemaphoreType.DMA((CHUNKS, 3)),
            pltpu.SemaphoreType.DMA,
            pltpu.SemaphoreType.DMA,
        ],
        compiler_params=pltpu.CompilerParams(
            collective_id=0, has_side_effects=True, vmem_limit_bytes=48 * 1024 * 1024
        ),
    )(t2_amps, v_slab, ij_irrep[None, :], ab_irrep[None, :], cd_irrep[None, :], cd_irrep.reshape(CD // 128, 128))


def dense_path(t2_amps, v_slab, ij_irrep, ab_irrep, cd_irrep):
    t2_sym = t2_amps * (ij_irrep[:, None] == cd_irrep[None, :]).astype(F32)
    v_sym = v_slab * (ab_irrep[:, None] == cd_irrep[None, :]).astype(F32)
    gathered = t2_sym
    hop = 1
    while hop < NAB:
        moved = lax.ppermute(gathered, "ab", [(i, (i + hop) % NAB) for i in range(NAB)])
        gathered = jnp.concatenate([moved, gathered], axis=0)
        hop *= 2
    me, x = lax.axis_index("ab"), lax.axis_index("cd")
    gathered = jnp.roll(gathered, (me + 1) * ROWS, axis=0)
    partial = lax.dot_general(
        gathered, v_sym, (((1,), (1,)), ((), ())), precision=lax.Precision.HIGHEST, preferred_element_type=F32
    )
    parts = jnp.transpose(partial.reshape(NAB, NX, ROWS // NX, AB), (1, 0, 2, 3))
    summed = lax.dynamic_index_in_dim(parts, x, 0, keepdims=False)
    for d in range(1, NX):
        theirs = lax.dynamic_index_in_dim(parts, (x + d) % NX, 0, keepdims=False)
        summed = summed + lax.ppermute(theirs, "cd", [(i, (i + d) % NX) for i in range(NX)])
    return lax.all_to_all(summed.reshape(NAB * ROWS // NX, AB), "ab", split_axis=0, concat_axis=1, tiled=True)


def on_device(t2_amps, v_slab, ij_irrep, ab_irrep, cd_irrep):
    rows, most = compact(t2_amps, v_slab, ij_irrep, ab_irrep, cd_irrep)

    def finish(rows, *_):
        return jnp.transpose(rows, (1, 0, 2)).reshape(4, NAB * AB)

    def dense(_, *args):
        return dense_path(*args)

    return lax.cond(
        most[0, 0] >= SLOTS, dense, finish, rows, t2_amps, v_slab, ij_irrep, ab_irrep, cd_irrep
    )


def solution(mesh):
    in_specs = (P("ab", "cd"), P("ab", "cd"), P("ab"), P("ab"), P("cd"))
    return jax.shard_map(on_device, mesh=mesh, in_specs=in_specs, out_specs=P(("ab", "cd"), None), check_vma=False)
```

time: 94.7 us -> 83.1 us (0.88)
  Pallas kernels: 86.9 us -> 80.4 us
  local copies, waits for them, and re-layouts: 4.17 us -> 1.57 us
  other arithmetic: 2.28 us -> 0 us
    pallas_call x1, Pallas kernels: 86.9 us -> 80.4 us  [compact(): pl.pallas_call(kernel, out_shape=(jax.ShapeDtypeStruct((NAB, 4, AB), F32)...]
    reshape x3 -> x0, local copies, waits for them, and re-layouts: 1.92 us -> none  [the longest x1 1.02 us: finish(): return jnp.transpose(tiles, (2, 0, 3, 1, 4)).reshape(4, NAB * AB)]
    concatenate x1 -> x0, other arithmetic: 1.57 us -> none  [compact(): block = jnp.concatenate([t2_amps, labels], axis=1)]
where the time goes in v2:
time: 83.1 us; the launch traced here: 82.9 us
  Pallas kernels  80.4 us (97%)
  local copies, waits for them, and re-layouts  1.57 us (2%)
    pallas_call x1, Pallas kernels, compact(): pl.pallas_call(kernel, out_shape=(jax.ShapeDtypeStruct((NAB, 4, AB), F32)...  80.4 us

profile of v2, /device:TPU:1, one launch (start us, length us, event | category | flops | bytes accessed | tf_op | source)
XLA Modules:
  0.0 82.9 jit_solution(6624515348323354226)
XLA Ops:
  0.0 0.0 copy-start.5
  0.0 0.0 copy-start.6
  0.0 0.0 copy-start.7
  0.0 0.0 copy-start.2
  0.0 80.4 %shard_map.57 = (f32[64,4,1024]{2,1,0:T(4,128)S(1)}, f32[8,128]{1,0:T(8,128)S(1)}) custom-call(f32[16,2048]{1,0:T(8,128)} %t2_ref.1, f32[1024,2048]{1,0:T(8,128)} %v_ref.1, s32[1,16]{1,0:T(1,128)} %bitcast.37, s32[1,1024]{1,0:T(1,128)} %bitcast.38, s32[1,2048]{1,0:T(1,128)} %bitcast.35, s32[16,128]{1,0:T(8,128)} %bitcast.36), custom_call_target="tpu_custom_call" | custom-call | tf_op jit(solution)/shard_map/pallas_call | solution.py:349
  80.4 0.1 copy.60
  80.5 0.5 slice.3
  81.7 0.0 copy-done.5
  81.7 0.0 copy-done.6
  81.7 0.0 copy-done.7
  81.7 0.0 copy-done.2
  81.7 0.2 conditional.1
  81.9 1.0 %copy.61 = f32[4,65536]{1,0:T(4,128)} copy(f32[4,65536]{1,0:T(4,128)S(1)} %get-tuple-element.28) | data formatting | bytes 2097152
Async XLA Ops:
  0.0 81.7 %copy-start.5 = (s32[2048]{0:T(1024)S(1)}, s32[2048]{0:T(1024)}, u32[]{:S(2)}) copy-start(s32[2048]{0:T(1024)} %param.11) | copy-start | bytes 24580
  0.0 81.7 %copy-start.6 = (s32[16]{0:T(128)S(1)}, s32[16]{0:T(128)}, u32[]{:S(2)}) copy-start(s32[16]{0:T(128)} %param.9) | copy-start | bytes 196
  0.0 81.7 %copy-start.7 = (s32[1024]{0:T(1024)S(1)}, s32[1024]{0:T(1024)}, u32[]{:S(2)}) copy-start(s32[1024]{0:T(1024)} %param.10) | copy-start | bytes 12292
  0.0 81.7 %copy-start.2 = (f32[16,2048]{1,0:T(8,128)S(1)}, f32[16,2048]{1,0:T(8,128)}, u32[]{:S(2)}) copy-start(f32[16,2048]{1,0:T(8,128)} %t2_ref.1) | copy-start | bytes 393220

commit v3 on v2

--- a/solution.py
+++ b/solution.py
@@ -14,21 +14,47 @@
 AB = 1024
 SLOTS = 72
 LEAD = 40
-CHUNKS = 4
-WIDTH = AB // CHUNKS
+WIDTHS = (128, 256, 256, 384)
+STARTS = tuple(sum(WIDTHS[:q]) for q in range(len(WIDTHS)))
+CHUNKS = len(WIDTHS)
 VROWS = 64
 GROUP = NAB * 4
 F32, BF16 = jnp.float32, jnp.bfloat16
 MESH = pl.DeviceIdType.MESH
 EARLY = 10
+SLOT_TIMES = (30, 38, 46, 54)
 SPAN = {"a": (0, 24, LEAD), "b": (LEAD, 56, SLOTS)}
+LAST = {"z": 4, "y": 2}
+FIRST = {"z": (1, 2), "y": (1, 2)}
+HOPS = {("z", 1): 1, ("z", 2): 2, ("z", 3): 1, ("z", 4): 2, ("y", 1): 1, ("y", 2): 2}
 
 
 def span(part, step, axis, sign):
     low, middle, high = SPAN[part]
-    if step < (4 if axis == "z" else 2):
+    if step < LAST[axis]:
         return low, high - low
     return (low, middle - low) if sign == 1 else (middle, high - middle)
+
+
+def follow(item, whole):
+    part, axis, offset, sign, step = item
+    onward = [(part, axis, offset, sign, n) for n in (3, 4)] if (axis, step) == ("z", 2) else []
+    turn = None
+    if (part == "a") == (axis == "z"):
+        if step < LAST[axis]:
+            turn = -sign * step
+        else:
+            whole[part] = whole.get(part, 0) + 1
+            if whole[part] == 2:
+                turn = LAST[axis]
+    return onward, [] if turn is None else opening(part, turn, "y" if axis == "z" else "z")
+
+
+def opening(part, offset, axis):
+    return [(part, axis, offset, sign, step) for step in FIRST[axis] for sign in (1, -1)]
+
+
+START = opening("a", 0, "z") + opening("b", 0, "y") + opening("b", 0, "z") + opening("a", 0, "y")
 
 
 def pieces():
@@ -40,33 +66,19 @@
         part, axis, _, sign, step = item
         link = axis + str(sign)
         start = max(free.get(link, 0.0), now)
-        free[link] = start + span(part, step, axis, sign)[1] * 0.0111
-        queue.append((free[link] + 1.8, len(order) + len(queue), item))
-
-    def first(now, part, offset, axis):
-        for sign in (1, -1):
-            issue(now, (part, axis, offset, sign, 1))
-
-    first(0.0, "a", 0, "z")
-    first(0.0, "b", 0, "y")
-    first(0.0, "b", 0, "z")
-    first(0.0, "a", 0, "y")
+        free[link] = start + span(part, step, axis, sign)[1] * 0.0111 * HOPS[axis, step]
+        queue.append((free[link] + 1.1 + 0.7 * HOPS[axis, step], len(order) + len(queue), item))
+
+    for item in START:
+        issue(0.0, item)
     whole = {}
     while queue:
         queue.sort()
         now, _, item = queue.pop(0)
         order.append(item)
-        part, axis, offset, sign, step = item
-        last = 4 if axis == "z" else 2
-        if step < last:
-            issue(now, (part, axis, offset, sign, step + 1))
-        if (part == "a") == (axis == "z"):
-            if step < last:
-                first(now, part, -sign * step, "y" if axis == "z" else "z")
-            else:
-                whole[part] = whole.get(part, 0) + 1
-                if whole[part] == 2:
-                    first(now, part, last, "y" if axis == "z" else "z")
+        for group in follow(item, whole):
+            for more in group:
+                issue(now, more)
     return order
 
 
@@ -107,18 +119,18 @@
         return ((zz % NZ) * NY + yy % NY) * NR + rr
 
     def peer(d):
-        return z + d // 8, y + (d // 2) % 4, (r + d % 2) % 2
+        return lax.rem(ab + d, NAB)
 
     load = pltpu.make_async_copy(t2_ref, amps, own_sem.at[0])
     load.start()
 
     def v_copy(n):
-        return pltpu.make_async_copy(v_ref.at[pl.ds(n * VROWS, VROWS)], vbuf.at[n % 3], v_sem.at[n % 3])
+        return pltpu.make_async_copy(v_ref.at[pl.ds(n * VROWS, VROWS)], vbuf.at[n], v_sem.at[n])
 
     barrier = pltpu.get_barrier_semaphore()
 
     def greet(d, carry):
-        pl.semaphore_signal(barrier, inc=1, device_id=(name(*peer(d)), x), device_id_type=MESH)
+        pl.semaphore_signal(barrier, inc=1, device_id=(peer(d), x), device_id_type=MESH)
         return carry
 
     lax.fori_loop(1, NAB, greet, 0)
@@ -128,30 +140,29 @@
     mine[...] = jnp.full((1, 128), -1, jnp.int32)
     mine[:, :ROWS] = ij_ref[...]
     load.wait()
-    for n in range(2):
+    for n in range(AB // VROWS):
         v_copy(n).start()
-    for c in range(NX):
-        amps4[c] = amps[4 * c : 4 * c + 4, :]
+    for to in range(NAB):
+        chunk = (to // 8) * 2 + to % 2
+        c = (to // 2) % 4
+        amps4[to] = amps[4 * c : 4 * c + 4, chunk * 128 : (chunk + 1) * 128]
     pl.semaphore_wait(barrier, NAB - 1 + NX - 1)
 
     def scatter(d, carry):
-        zz, yy, rr = peer(d)
-        zz, yy = zz % NZ, yy % NY
-        to = (name(zz, yy, rr), x)
+        there = peer(d)
+        to = (there, x)
         pltpu.make_async_remote_copy(
             src_ref=mine, dst_ref=labels.at[ab], send_sem=s_send.at[0], recv_sem=l_recv, device_id=to, device_id_type=MESH
         ).start()
         pltpu.make_async_remote_copy(
-            src_ref=amps4.at[yy, :, pl.ds(pl.multiple_of((zz * 2 + rr) * 128, 128), 128)], dst_ref=rows4.at[ab],
+            src_ref=amps4.at[there], dst_ref=rows4.at[ab],
             send_sem=s_send.at[1], recv_sem=q_recv, device_id=to, device_id_type=MESH,
         ).start()
         return carry
 
     lax.fori_loop(1, NAB, scatter, 0)
     keep_label = pltpu.make_async_copy(mine, labels.at[ab], own_sem.at[1])
-    keep_rows = pltpu.make_async_copy(
-        amps4.at[y, :, pl.ds(pl.multiple_of((z * 2 + r) * 128, 128), 128)], rows4.at[ab], own_sem.at[2]
-    )
+    keep_rows = pltpu.make_async_copy(amps4.at[ab], rows4.at[ab], own_sem.at[2])
     keep_label.start()
     keep_rows.start()
 
@@ -160,11 +171,9 @@
     abcol[...] = column(ab_row)
 
     def v_step(n):
-        if n + 2 < AB // VROWS:
-            v_copy(n + 2).start()
         v_copy(n).wait()
         keep = abcol[n * VROWS : (n + 1) * VROWS, :1] == cd_row
-        hi, lo = split2(jnp.where(keep, vbuf[n % 3], 0.0))
+        hi, lo = split2(jnp.where(keep, vbuf[n], 0.0))
         vhi[n * VROWS : (n + 1) * VROWS, :] = hi
         vlo[n * VROWS : (n + 1) * VROWS, :] = lo
 
@@ -204,12 +213,13 @@
     def sent(item):
         part_, axis, offset, sign, step = item
         low, count = span(part_, step, axis, sign)
+        hop = HOPS[axis, step]
         if axis == "z":
-            source = name(z + 16 - sign * (step - 1), y + 8 + offset, r)
-            target = name(z + 16 + sign, y, r)
+            source = name(z + 16 - sign * (step - hop), y + 8 + offset, r)
+            target = name(z + 16 + sign * hop, y, r)
         else:
-            source = name(z + 16 + offset, y + 8 - sign * (step - 1), r)
-            target = name(z, y + 8 + sign, r)
+            source = name(z + 16 + offset, y + 8 - sign * (step - hop), r)
+            target = name(z, y + 8 + sign * hop, r)
         ref = g.at[source, pl.ds(low, count)]
         return pltpu.make_async_remote_copy(
             src_ref=ref, dst_ref=ref, send_sem=send_sem, recv_sem=recv_sem.at[INDEX[item]],
@@ -234,50 +244,36 @@
             device_id=(name(z, y, 1 - r), x), device_id_type=MESH,
         ).start()
 
-    def first(part_, offset, axis):
-        for sign in (1, -1):
-            sent((part_, axis, offset, sign, 1)).start()
-
-    first("a", 0, "z")
-    first("b", 0, "y")
-    first("b", 0, "z")
-    first("a", 0, "y")
+    for item in START:
+        sent(item).start()
     give(ab, pl.ds(0, SLOTS))
 
     most = jnp.zeros((1, 128), F32)
     my_label = jnp.zeros((GROUP, 128), F32)
     my_slot = jnp.zeros((GROUP, 128), F32)
-    for c in range(NX):
-        label, slot = slots_of(c)
-        most = jnp.maximum(most, jnp.max(slot, axis=0, keepdims=True))
-        my_label = jnp.where(x == c, label, my_label)
-        my_slot = jnp.where(x == c, slot, my_slot)
-    flag_ref[...] = jnp.broadcast_to(most, (8, 128))
-    spread = (my_slot[:, :SLOTS] == lane_i[:, :SLOTS].astype(F32)).astype(BF16)
-
     steps = AB // VROWS
     done = EARLY
     whole = {}
     for count, item in enumerate(ORDER):
-        part_, axis, offset, sign, step = item
         source, rows = arrived(item)
-        last = 4 if axis == "z" else 2
-        if step < last:
-            sent((part_, axis, offset, sign, step + 1)).start()
-        if (part_ == "a") == (axis == "z"):
-            if step < last:
-                first(part_, -sign * step, "y" if axis == "z" else "z")
-            else:
-                whole[part_] = whole.get(part_, 0) + 1
-                if whole[part_] == 2:
-                    first(part_, last, "y" if axis == "z" else "z")
+        for group in follow(item, whole):
+            for more in group:
+                sent(more).start()
         give(source, rows)
+        if count in SLOT_TIMES:
+            c = SLOT_TIMES.index(count)
+            label, slot = slots_of(c)
+            most = jnp.maximum(most, jnp.max(slot, axis=0, keepdims=True))
+            my_label = jnp.where(x == c, label, my_label)
+            my_slot = jnp.where(x == c, slot, my_slot)
         while done < steps and (done - EARLY) * (len(ORDER) - 16) < count * (steps - EARLY):
             v_step(done)
             done += 1
     while done < steps:
         v_step(done)
         done += 1
+    flag_ref[0, 0] = jnp.where(jnp.max(most) >= SLOTS, 1, 0)
+    spread = (my_slot[:, :SLOTS] == lane_i[:, :SLOTS].astype(F32)).astype(BF16)
     pltpu.make_async_copy(g.at[pl.ds(0, 32)], g.at[pl.ds(0, 32)], mate_sem).wait()
 
     for k in range(CD // 128):
@@ -286,46 +282,49 @@
         chi[: NX * SLOTS, k * 128 : (k + 1) * 128] = hi
         chi[NX * SLOTS :, k * 128 : (k + 1) * 128] = lo
 
+    def columns(q):
+        return pl.ds(STARTS[q], WIDTHS[q])
+
     def x_copy(q, d):
         to = (x + d) % NX
         return pltpu.make_async_remote_copy(
-            src_ref=part.at[q, to], dst_ref=landed.at[q, d - 1], send_sem=x_send.at[q, d - 1],
+            src_ref=part.at[to, :, columns(q)], dst_ref=landed.at[d - 1, :, columns(q)], send_sem=x_send.at[q, d - 1],
             recv_sem=x_recv.at[q, d - 1], device_id=(ab, to), device_id_type=MESH,
         )
 
     def product(q):
-        cols = slice(q * WIDTH, (q + 1) * WIDTH)
+        cols = slice(STARTS[q], STARTS[q] + WIDTHS[q])
         both = dot_nt(chi[...], vhi[cols, :])
         cross = dot_nt(chi[: NX * SLOTS, :], vlo[cols, :])
         total = both[: NX * SLOTS] + both[NX * SLOTS :] + cross
         for c in range(NX):
-            part[q, c] = total[c * SLOTS : (c + 1) * SLOTS]
+            part[c, :, cols] = total[c * SLOTS : (c + 1) * SLOTS]
         for d in (2, 1, 3):
             x_copy(q, d).start()
 
     ab_f = ab_row.astype(F32)
 
     def exchange(q):
-        cols = slice(q * WIDTH, (q + 1) * WIDTH)
+        cols = slice(STARTS[q], STARTS[q] + WIDTHS[q])
         for d in (1, 3, 2):
             x_copy(q, d).wait_recv()
-        total = part[q, x] + landed[q, 0] + landed[q, 1] + landed[q, 2]
+        total = part[x, :, cols] + landed[0, :, cols] + landed[1, :, cols] + landed[2, :, cols]
         hi = total.astype(BF16)
         mid, lo = split2(total - hi.astype(F32))
         rows = dot(spread, hi) + dot(spread, mid) + dot(spread, lo)
         rows = jnp.where(my_label[:, :1] == ab_f[:, cols], rows, 0.0)
-        dense[q] = rows.reshape(NAB, 4, WIDTH)
+        dense[:, :, cols] = rows.reshape(NAB, 4, WIDTHS[q])
 
         def send(d, carry):
-            to = name(*peer(d))
+            to = peer(d)
             pltpu.make_async_remote_copy(
-                src_ref=dense.at[q, to], dst_ref=out_ref.at[ab, :, pl.ds(q * WIDTH, WIDTH)], send_sem=a_send,
+                src_ref=dense.at[to, :, columns(q)], dst_ref=out_ref.at[ab, :, columns(q)], send_sem=a_send,
                 recv_sem=a_recv, device_id=(to, x), device_id_type=MESH,
             ).start()
             return carry
 
         lax.fori_loop(1, NAB, send, 0)
-        out_ref[ab, :, cols] = dense[q, ab]
+        out_ref[ab, :, cols] = dense[ab, :, cols]
 
     product(0)
     for q in range(CHUNKS):
@@ -348,26 +347,26 @@
     hbm = pl.BlockSpec(memory_space=pl.ANY)
     return pl.pallas_call(
         kernel,
-        out_shape=(jax.ShapeDtypeStruct((NAB, 4, AB), F32), jax.ShapeDtypeStruct((8, 128), F32)),
+        out_shape=(jax.ShapeDtypeStruct((NAB, 4, AB), F32), jax.ShapeDtypeStruct((1, 1), jnp.int32)),
         in_specs=[hbm, hbm, vmem, vmem, vmem, vmem],
-        out_specs=(vmem, vmem),
+        out_specs=(vmem, pl.BlockSpec(memory_space=pltpu.SMEM)),
         scratch_shapes=[
             pltpu.VMEM((ROWS, CD), F32),
-            pltpu.VMEM((NX, 4, CD), F32),
+            pltpu.VMEM((NAB, 4, 128), F32),
             pltpu.VMEM((1, 128), jnp.int32),
             pltpu.VMEM((NAB, 1, 128), jnp.int32),
             pltpu.VMEM((NAB, 4, 128), F32),
             pltpu.VMEM((NAB, SLOTS, 128), F32),
-            pltpu.VMEM((3, VROWS, CD), F32),
+            pltpu.VMEM((AB // VROWS, VROWS, CD), F32),
             pltpu.VMEM((AB, CD), BF16),
             pltpu.VMEM((AB, CD), BF16),
             pltpu.VMEM((AB, 128), jnp.int32),
             pltpu.VMEM((2 * NX * SLOTS, CD), BF16),
-            pltpu.VMEM((CHUNKS, NX, SLOTS, WIDTH), F32),
-            pltpu.VMEM((CHUNKS, NX - 1, SLOTS, WIDTH), F32),
-            pltpu.VMEM((CHUNKS, NAB, 4, WIDTH), F32),
+            pltpu.VMEM((NX, SLOTS, AB), F32),
+            pltpu.VMEM((NX - 1, SLOTS, AB), F32),
+            pltpu.VMEM((NAB, 4, AB), F32),
             pltpu.SemaphoreType.DMA((3,)),
-            pltpu.SemaphoreType.DMA((3,)),
+            pltpu.SemaphoreType.DMA((AB // VROWS,)),
             pltpu.SemaphoreType.DMA((2,)),
             pltpu.SemaphoreType.DMA,
             pltpu.SemaphoreType.DMA,
@@ -408,7 +407,7 @@
 
 
 def on_device(t2_amps, v_slab, ij_irrep, ab_irrep, cd_irrep):
-    rows, most = compact(t2_amps, v_slab, ij_irrep, ab_irrep, cd_irrep)
+    rows, over = compact(t2_amps, v_slab, ij_irrep, ab_irrep, cd_irrep)
 
     def finish(rows, *_):
         return jnp.transpose(rows, (1, 0, 2)).reshape(4, NAB * AB)
@@ -417,7 +416,7 @@
         return dense_path(*args)
 
     return lax.cond(
-        most[0, 0] >= SLOTS, dense, finish, rows, t2_amps, v_slab, ij_irrep, ab_irrep, cd_irrep
+        over[0, 0] > 0, dense, finish, rows, t2_amps, v_slab, ij_irrep, ab_irrep, cd_irrep
     )
 
 

time: 83.1 us -> 73.5 us (0.88)
  Pallas kernels: 80.4 us -> 71.4 us
    pallas_call x1, Pallas kernels: 80.4 us -> 71.4 us  [compact(): pl.pallas_call(kernel, out_shape=(jax.ShapeDtypeStruct((NAB, 4, AB), F32)...]
where the time goes in v3:
time: 73.5 us; the launch traced here: 73.3 us
  Pallas kernels  71.4 us (97%)
  local copies, waits for them, and re-layouts  1.06 us (1%)
    pallas_call x1, Pallas kernels, compact(): pl.pallas_call(kernel, out_shape=(jax.ShapeDtypeStruct((NAB, 4, AB), F32)...  71.4 us

profile of v3, /device:TPU:1, one launch (start us, length us, event | category | flops | bytes accessed | tf_op | source)
XLA Modules:
  0.0 73.3 jit_solution(16535870652216512042)
XLA Ops:
  0.0 0.0 copy-start.5
  0.0 0.0 copy-start.6
  0.0 0.0 copy-start.7
  0.0 0.0 copy-start.2
  0.0 71.4 %shard_map.57 = (f32[64,4,1024]{2,1,0:T(4,128)S(1)}, s32[1,1]{1,0:T(1,128)}) custom-call(f32[16,2048]{1,0:T(8,128)} %t2_ref.1, f32[1024,2048]{1,0:T(8,128)} %v_ref.1, s32[1,16]{1,0:T(1,128)} %bitcast.37, s32[1,1024]{1,0:T(1,128)} %bitcast.38, s32[1,2048]{1,0:T(1,128)} %bitcast.35, s32[16,128]{1,0:T(8,128)} %bitcast.36), custom_call_target="tpu_custom_call" | custom-call | tf_op jit(solution)/shard_map/pallas_call | solution.py:348
  71.4 0.1 copy.60
  72.1 0.0 copy-done.5
  72.1 0.0 copy-done.6
  72.1 0.0 copy-done.7
  72.1 0.0 copy-done.2
  72.1 0.2 conditional.1
  72.4 1.0 %copy.61 = f32[4,65536]{1,0:T(4,128)} copy(f32[4,65536]{1,0:T(4,128)S(1)} %get-tuple-element.28) | data formatting | bytes 2097152
Async XLA Ops:
  0.0 72.1 %copy-start.5 = (s32[2048]{0:T(1024)S(1)}, s32[2048]{0:T(1024)}, u32[]{:S(2)}) copy-start(s32[2048]{0:T(1024)} %param.11) | copy-start | bytes 24580
  0.0 72.1 %copy-start.6 = (s32[16]{0:T(128)S(1)}, s32[16]{0:T(128)}, u32[]{:S(2)}) copy-start(s32[16]{0:T(128)} %param.9) | copy-start | bytes 196
  0.0 72.1 %copy-start.7 = (s32[1024]{0:T(1024)S(1)}, s32[1024]{0:T(1024)}, u32[]{:S(2)}) copy-start(s32[1024]{0:T(1024)} %param.10) | copy-start | bytes 12292
  0.0 72.1 %copy-start.2 = (f32[16,2048]{1,0:T(8,128)S(1)}, f32[16,2048]{1,0:T(8,128)}, u32[]{:S(2)}) copy-start(f32[16,2048]{1,0:T(8,128)} %t2_ref.1) | copy-start | bytes 393220

commit v4 on v3

--- a/solution.py
+++ b/solution.py
@@ -118,6 +118,16 @@
     def name(zz, yy, rr):
         return ((zz % NZ) * NY + yy % NY) * NR + rr
 
+    def to_all(send):
+        send(peer(NAB // 2))
+
+        def two(n, carry):
+            send(peer(NAB // 2 - 1 - n))
+            send(peer(NAB - (NAB // 2 - 1 - n)))
+            return carry
+
+        lax.fori_loop(0, NAB // 2 - 1, two, 0)
+
     def peer(d):
         return lax.rem(ab + d, NAB)
 
@@ -129,11 +139,7 @@
 
     barrier = pltpu.get_barrier_semaphore()
 
-    def greet(d, carry):
-        pl.semaphore_signal(barrier, inc=1, device_id=(peer(d), x), device_id_type=MESH)
-        return carry
-
-    lax.fori_loop(1, NAB, greet, 0)
+    to_all(lambda there: pl.semaphore_signal(barrier, inc=1, device_id=(there, x), device_id_type=MESH))
     for d in (1, 2, 3):
         pl.semaphore_signal(barrier, inc=1, device_id=(ab, (x + d) % NX), device_id_type=MESH)
 
@@ -148,8 +154,7 @@
         amps4[to] = amps[4 * c : 4 * c + 4, chunk * 128 : (chunk + 1) * 128]
     pl.semaphore_wait(barrier, NAB - 1 + NX - 1)
 
-    def scatter(d, carry):
-        there = peer(d)
+    def scatter(there):
         to = (there, x)
         pltpu.make_async_remote_copy(
             src_ref=mine, dst_ref=labels.at[ab], send_sem=s_send.at[0], recv_sem=l_recv, device_id=to, device_id_type=MESH
@@ -158,9 +163,8 @@
             src_ref=amps4.at[there], dst_ref=rows4.at[ab],
             send_sem=s_send.at[1], recv_sem=q_recv, device_id=to, device_id_type=MESH,
         ).start()
-        return carry
-
-    lax.fori_loop(1, NAB, scatter, 0)
+
+    to_all(scatter)
     keep_label = pltpu.make_async_copy(mine, labels.at[ab], own_sem.at[1])
     keep_rows = pltpu.make_async_copy(amps4.at[ab], rows4.at[ab], own_sem.at[2])
     keep_label.start()
@@ -315,15 +319,13 @@
         rows = jnp.where(my_label[:, :1] == ab_f[:, cols], rows, 0.0)
         dense[:, :, cols] = rows.reshape(NAB, 4, WIDTHS[q])
 
-        def send(d, carry):
-            to = peer(d)
+        def send(to):
             pltpu.make_async_remote_copy(
                 src_ref=dense.at[to, :, columns(q)], dst_ref=out_ref.at[ab, :, columns(q)], send_sem=a_send,
                 recv_sem=a_recv, device_id=(to, x), device_id_type=MESH,
             ).start()
-            return carry
-
-        lax.fori_loop(1, NAB, send, 0)
+
+        to_all(send)
         out_ref[ab, :, cols] = dense[ab, :, cols]
 
     product(0)

time: 73.5 us -> 72.7 us (0.989)
  Pallas kernels: 71.4 us -> 70.6 us
    pallas_call x1, Pallas kernels: 71.4 us -> 70.6 us  [compact(): pl.pallas_call(kernel, out_shape=(jax.ShapeDtypeStruct((NAB, 4, AB), F32)...]
where the time goes in v4:
time: 72.7 us; the launch traced here: 72.6 us
  Pallas kernels  70.6 us (97%)
  local copies, waits for them, and re-layouts  1.06 us (1%)
    pallas_call x1, Pallas kernels, compact(): pl.pallas_call(kernel, out_shape=(jax.ShapeDtypeStruct((NAB, 4, AB), F32)...  70.6 us

profile of v4, /device:TPU:1, one launch (start us, length us, event | category | flops | bytes accessed | tf_op | source)
XLA Modules:
  0.0 72.6 jit_solution(15170510090918765028)
XLA Ops:
  0.0 0.0 copy-start.5
  0.0 0.0 copy-start.6
  0.0 0.0 copy-start.7
  0.0 0.0 copy-start.2
  0.0 70.6 %shard_map.57 = (f32[64,4,1024]{2,1,0:T(4,128)S(1)}, s32[1,1]{1,0:T(1,128)}) custom-call(f32[16,2048]{1,0:T(8,128)} %t2_ref.1, f32[1024,2048]{1,0:T(8,128)} %v_ref.1, s32[1,16]{1,0:T(1,128)} %bitcast.37, s32[1,1024]{1,0:T(1,128)} %bitcast.38, s32[1,2048]{1,0:T(1,128)} %bitcast.35, s32[16,128]{1,0:T(8,128)} %bitcast.36), custom_call_target="tpu_custom_call" | custom-call | tf_op jit(solution)/shard_map/pallas_call | solution.py:350
  70.6 0.1 copy.60
  71.3 0.0 copy-done.5
  71.4 0.0 copy-done.6
  71.4 0.0 copy-done.7
  71.4 0.0 copy-done.2
  71.4 0.2 conditional.1
  71.6 1.0 %copy.61 = f32[4,65536]{1,0:T(4,128)} copy(f32[4,65536]{1,0:T(4,128)S(1)} %get-tuple-element.28) | data formatting | bytes 2097152
Async XLA Ops:
  0.0 71.4 %copy-start.5 = (s32[2048]{0:T(1024)S(1)}, s32[2048]{0:T(1024)}, u32[]{:S(2)}) copy-start(s32[2048]{0:T(1024)} %param.11) | copy-start | bytes 24580
  0.0 71.4 %copy-start.6 = (s32[16]{0:T(128)S(1)}, s32[16]{0:T(128)}, u32[]{:S(2)}) copy-start(s32[16]{0:T(128)} %param.9) | copy-start | bytes 196
  0.0 71.4 %copy-start.7 = (s32[1024]{0:T(1024)S(1)}, s32[1024]{0:T(1024)}, u32[]{:S(2)}) copy-start(s32[1024]{0:T(1024)} %param.10) | copy-start | bytes 12292
  0.0 71.4 %copy-start.2 = (f32[16,2048]{1,0:T(8,128)S(1)}, f32[16,2048]{1,0:T(8,128)}, u32[]{:S(2)}) copy-start(f32[16,2048]{1,0:T(8,128)} %t2_ref.1) | copy-start | bytes 393220

commit v5 on v4

--- a/solution.py
+++ b/solution.py
@@ -14,7 +14,7 @@
 AB = 1024
 SLOTS = 72
 LEAD = 40
-WIDTHS = (128, 256, 256, 384)
+WIDTHS = (128, 256, 384, 256)
 STARTS = tuple(sum(WIDTHS[:q]) for q in range(len(WIDTHS)))
 CHUNKS = len(WIDTHS)
 VROWS = 64

time: 72.7 us -> 73 us (level)
  no operation moved by 1% of the time
where the time goes in v5:
time: 73 us; the launch traced here: 72.9 us
  Pallas kernels  70.9 us (97%)
  local copies, waits for them, and re-layouts  1.06 us (1%)
    pallas_call x1, Pallas kernels, compact(): pl.pallas_call(kernel, out_shape=(jax.ShapeDtypeStruct((NAB, 4, AB), F32)...  70.9 us

profile of v5, /device:TPU:1, one launch (start us, length us, event | category | flops | bytes accessed | tf_op | source)
XLA Modules:
  0.0 72.9 jit_solution(3139554425377698972)
XLA Ops:
  0.0 0.0 copy-start.5
  0.0 0.0 copy-start.6
  0.0 0.0 copy-start.7
  0.0 0.0 copy-start.2
  0.0 70.9 %shard_map.57 = (f32[64,4,1024]{2,1,0:T(4,128)S(1)}, s32[1,1]{1,0:T(1,128)}) custom-call(f32[16,2048]{1,0:T(8,128)} %t2_ref.1, f32[1024,2048]{1,0:T(8,128)} %v_ref.1, s32[1,16]{1,0:T(1,128)} %bitcast.37, s32[1,1024]{1,0:T(1,128)} %bitcast.38, s32[1,2048]{1,0:T(1,128)} %bitcast.35, s32[16,128]{1,0:T(8,128)} %bitcast.36), custom_call_target="tpu_custom_call" | custom-call | tf_op jit(solution)/shard_map/pallas_call | solution.py:350
  71.0 0.1 copy.60
  71.7 0.0 copy-done.5
  71.7 0.0 copy-done.6
  71.7 0.0 copy-done.7
  71.7 0.0 copy-done.2
  71.7 0.2 conditional.1
  71.9 1.0 %copy.61 = f32[4,65536]{1,0:T(4,128)} copy(f32[4,65536]{1,0:T(4,128)S(1)} %get-tuple-element.28) | data formatting | bytes 2097152
Async XLA Ops:
  0.0 71.7 %copy-start.5 = (s32[2048]{0:T(1024)S(1)}, s32[2048]{0:T(1024)}, u32[]{:S(2)}) copy-start(s32[2048]{0:T(1024)} %param.11) | copy-start | bytes 24580
  0.0 71.7 %copy-start.6 = (s32[16]{0:T(128)S(1)}, s32[16]{0:T(128)}, u32[]{:S(2)}) copy-start(s32[16]{0:T(128)} %param.9) | copy-start | bytes 196
  0.0 71.7 %copy-start.7 = (s32[1024]{0:T(1024)S(1)}, s32[1024]{0:T(1024)}, u32[]{:S(2)}) copy-start(s32[1024]{0:T(1024)} %param.10) | copy-start | bytes 12292
  0.0 71.7 %copy-start.2 = (f32[16,2048]{1,0:T(8,128)S(1)}, f32[16,2048]{1,0:T(8,128)}, u32[]{:S(2)}) copy-start(f32[16,2048]{1,0:T(8,128)} %t2_ref.1) | copy-start | bytes 393220
